TPU v7x, 32 devices: a whole 2x2x4 slice. The times are simulated.
32 devices in a mesh: rows: 8 (over y, x, core), feat: 4 (over z).
Axes of the slice: x: 2, y: 2, z: 4, core: 2. Of those that a mesh axis runs over, the one named last changes fastest.
Arguments:
- queries: bfloat16 [49152, 4096], P('rows', 'feat'), may hold values from -6 to 6
- projection: bfloat16 [4096, 128], P('feat'), may hold values from -0.09375 to 0.09375
- models: float32 [64, 128], replicated, may hold values from -0.5 to 0.5
- first: int32 [49152], P('rows'), may hold values from 0 to 63
- second: int32 [49152], P('rows'), may hold values from 0 to 63
- wins: int32 [49152], P('rows'), may hold values 0 or 1
Outputs:
- update_proj: float32 [4096, 128], P('feat')
- update_models: float32 [64, 128], replicated
- loss: float32 [], replicated
All inputs are finite; a program needn't handle non-finite values. No bound on the sum of `wins` on one device may be relied on, other than what follows from the above.
Results may differ from a plain program's by a relative error of at most 0.00045.
The roundings to bfloat16 on the way count: a program that leaves them out, or rounds other values in their place, can miss the bound.
Values may be sent and summed in bfloat16 or wider, within the bound.
A program may use at most 64 MiB of HBM per device.

v0:
```python
import jax
import jax.numpy as jnp
from jax import lax
from jax.sharding import PartitionSpec as P

D = 4096
R = 128
NM = 64


def pair_gap(models, first, second):
    return jnp.take(models, first, axis=0) - jnp.take(models, second, axis=0)


def pick_table(models, first, second):
    labels = jnp.arange(models.shape[0], dtype=jnp.int32)[:, None]
    return (labels == first[None, :]).astype(jnp.float32) - (labels == second[None, :]).astype(
        jnp.float32
    )


def body(queries, projection, models, first, second, wins):
    local_rows = queries.shape[0]
    total_rows = float(local_rows * lax.axis_size("rows"))
    partial_value = jnp.dot(queries, projection, preferred_element_type=jnp.float32)
    gap = pair_gap(models, first, second)
    margin = lax.psum(jnp.sum(partial_value * gap, axis=-1), "feat")
    sign = 2.0 * wins.astype(jnp.float32) - 1.0
    loss_part = jnp.sum(jax.nn.softplus(-sign * margin)) / total_rows
    coef = -sign * jax.nn.sigmoid(-sign * margin) / total_rows
    back = (coef[:, None] * gap).astype(jnp.bfloat16)
    pick = pick_table(models, first, second)
    model_part = jnp.dot(pick, coef[:, None] * partial_value, precision=lax.Precision.HIGHEST)
    feat_count = float(lax.axis_size("feat"))
    grad_models, loss = lax.psum((model_part, loss_part / feat_count), ("rows", "feat"))
    model_square = jnp.sum(grad_models * grad_models)
    entries = jnp.sqrt(jnp.float32(D * R + NM * R))
    grad_local = jnp.dot(queries.T, back, preferred_element_type=jnp.float32)
    grad_proj = lax.psum(grad_local, "rows")
    square = lax.psum(jnp.sum(grad_proj * grad_proj), "feat")
    scale = entries / (jnp.sqrt(square + model_square) + 1e-06)
    update_proj = scale * grad_proj
    return (update_proj, scale * grad_models, loss)


def solution(mesh):
    in_specs = (P("rows", "feat"), P("feat", None), P(), P("rows"), P("rows"), P("rows"))
    out_specs = (P("feat", None), P(), P())
    return jax.shard_map(body, mesh=mesh, in_specs=in_specs, out_specs=out_specs, check_vma=False)
```

profile of v0, /device:TPU:0, one launch (start us, length us, event | category | flops | bytes accessed | tf_op | source)
XLA Modules:
  0.0 177.5 jit_solution(17190203566094224995)
XLA Ops:
  7.2 0.0 copy-start
  7.2 0.0 copy-start.1
  7.2 0.0 all-reduce.3.cloned.1.call-start
  7.2 0.7 fusion.14
  8.0 0.8 compare_and_fusion
  8.8 0.7 fusion.13
  9.5 0.0 copy-done.1
  9.5 20.9 %gather_fusion.1 = f32[6144,128]{1,0:T(8,128)} fusion(f32[64,128]{1,0:T(8,128)S(1)} %copy-done.1, s32[6144]{0:T(1024)S(1)} %fusion.14), kind=kCustom, calls=%fused_computation.1.clone | custom fusion | bytes 6316032 | tf_op jit(solution)/shard_map/jit(_take)/gather | solution.py:12
  30.4 2.4 %copy.10 = f32[6144,128]{0,1:T(8,128)S(1)} copy(f32[6144,128]{1,0:T(8,128)} %gather_fusion.1) | data formatting | bytes 6291456 | tf_op jit(solution)/shard_map/jit(_take)/gather | solution.py:12
  32.8 20.9 %gather_fusion = f32[6144,128]{1,0:T(8,128)} fusion(f32[64,128]{1,0:T(8,128)S(1)} %copy-done.1, s32[6144]{0:T(1024)S(1)} %fusion.13), kind=kCustom, calls=%fused_computation.clone | custom fusion | bytes 6316032 | tf_op jit(solution)/shard_map/jit(_take)/gather | solution.py:12
  53.7 3.5 %copy.9 = f32[6144,128]{0,1:T(8,128)} copy(f32[6144,128]{1,0:T(8,128)} %gather_fusion) | data formatting | bytes 6291456 | tf_op jit(solution)/shard_map/jit(_take)/gather | solution.py:12
  57.2 0.0 copy-done
  57.2 0.0 copy-start.4
  57.2 11.7 %multiply_reduce_fusion = (f32[6144]{0:T(1024)S(1)}, f32[6144,128]{0,1:T(8,128)}) fusion(f32[6144,128]{0,1:T(8,128)S(1)} %copy.10, pred[6144]{0:T(1024)(128)(4,1)S(1)} %get-tuple-element.13, f32[6144,128]{0,1:T(8,128)} %copy.9, pred[6144]{0:T(1024)(128)(4,1)S(1)} %get-tuple-element.14, bf16[6144,1024]{1,0:T(8,128)(2,1)} %param.8, ...), kind=kOutput, calls=%fused_computation.6 | convolution fusion | flops 1614538752 | bytes 22319104 | tf_op jit(solution)/shard_map/dot_general | solution.py:25
  68.9 20.8 %psum.35 = f32[6144]{0:T(1024)S(1)} all-reduce(f32[6144]{0:T(1024)S(1)} %get-tuple-element.11), channel_id=1, replica_groups=mesh['rows'=8,'feat'=4] {'feat'}, use_global_device_ids=true, to_apply=%region_1.3 | all-reduce | flops 6144 | bytes 49152 | tf_op jit(solution)/shard_map/psum | solution.py:27
  89.6 0.0 copy-done.4
  89.6 0.6 fusion.11
  90.3 0.0 copy-start.2
  90.3 0.0 copy-start.3
  90.3 8.3 %fusion.8 = f32[1024,128]{0,1:T(8,128)} fusion(bf16[6144,1024]{1,0:T(8,128)(2,1)} %param.8, f32[6144]{0:T(1024)S(1)} %get-tuple-element.10, f32[6144,128]{0,1:T(8,128)S(1)} %copy.10, f32[6144,128]{0,1:T(8,128)} %copy.9, pred[6144]{0:T(1024)(128)(4,1)S(1)} %get-tuple-element.13, pred[6144]{0:T(1024)(128)(4,1)S(1)} %get-tuple-element.14), kind=kOutput, calls=%fused_computation.15 | convolution fusion | flops 1614544896 | bytes 19435520 | tf_op jit(solution)/shard_map/dot_general | solution.py:38
  98.6 0.0 all-reduce.3.cloned.1.call-update
  99.2 0.0 copy-done.2
  99.2 0.0 copy-done.3
  99.3 5.2 %fusion = f32[64,128]{1,0:T(8,128)S(1)} fusion(f32[6144,128]{0,1:T(8,128)} %get-tuple-element.12, f32[6144]{0:T(1024)S(1)} %get-tuple-element.10, s32[6144]{0:T(1024)S(1)} %copy-done.2, s32[6144]{0:T(1024)S(1)} %copy-done.3), kind=kOutput, calls=%fused_computation.3 | convolution fusion | flops 606732288 | bytes 3252224 | tf_op jit(solution)/shard_map/dot_general | solution.py:33
  104.4 38.9 %all-reduce = (f32[64,128]{1,0:T(8,128)S(1)}, f32[]{:T(128)}) all-reduce(f32[64,128]{1,0:T(8,128)S(1)} %fusion, f32[]{:T(128)S(6)} %div.20), channel_id=1, replica_groups=mesh['rows'=8,'feat'=4] {'rows','feat'}, use_global_device_ids=true, to_apply=%region_5.7 | all-reduce | flops 8193 | bytes 65544 | tf_op jit(solution)/shard_map/psum | solution.py:35
  143.3 8.6 %all-reduce.3.cloned.1.call-done = f32[1024,128]{0,1:T(8,128)} async-done(((f32[1024,128]{0,1:T(8,128)}), f32[1024,128]{0,1:T(8,128)}) %all-reduce.3.cloned.1.call-update) | async-done | bytes 524304 | tf_op jit(solution)/shard_map/psum | solution.py:39
  151.9 1.8 %multiply_reduce_fusion.1 = f32[]{:T(128)} fusion(f32[1024,128]{0,1:T(8,128)} %all-reduce.3.cloned.1.call-done), kind=kLoop, calls=%fused_computation.18 | loop fusion | flops 262143 | bytes 524292 | tf_op jit(solution)/shard_map/reduce_sum | solution.py:40
  153.7 0.6 multiply_reduce_fusion.2
  154.3 12.2 %psum.37 = f32[]{:T(128)} all-reduce(f32[]{:T(128)} %multiply_reduce_fusion.1), channel_id=1, replica_groups=mesh['rows'=8,'feat'=4] {'feat'}, use_global_device_ids=true, to_apply=%region_4.6 | all-reduce | flops 1 | bytes 8 | tf_op jit(solution)/shard_map/psum | solution.py:40
  168.0 0.6 broadcast_multiply_fusion.1
  168.6 1.1 broadcast_multiply_fusion
  169.7 1.0 copy.11
Async XLA Ops:
  7.2 50.0 %copy-start = (bf16[1024,128]{1,0:T(8,128)(2,1)S(1)}, bf16[1024,128]{1,0:T(8,128)(2,1)}, u32[]{:S(2)}) copy-start(bf16[1024,128]{1,0:T(8,128)(2,1)} %param.9) | copy-start | bytes 786436
  7.2 2.3 %copy-start.1 = (f32[64,128]{1,0:T(8,128)S(1)}, f32[64,128]{1,0:T(8,128)}, u32[]{:S(2)}) copy-start(f32[64,128]{1,0:T(8,128)} %param.10) | copy-start | bytes 98308
  7.2 144.8 %all-reduce.3.cloned.1.call-start = ((), (), s32[]{:S(2)}) async-start(), calls=%async_computation | async-start | bytes 1048576 | tf_op jit(solution)/shard_map/psum | solution.py:39
  57.2 32.4 %copy-start.4 = (s32[6144]{0:T(1024)S(1)}, s32[6144]{0:T(1024)}, u32[]{:S(2)}) copy-start(s32[6144]{0:T(1024)} %param.13) | copy-start | bytes 73732
  90.3 9.0 %copy-start.2 = (s32[6144]{0:T(1024)S(1)}, s32[6144]{0:T(1024)}, u32[]{:S(2)}) copy-start(s32[6144]{0:T(1024)} %param.12) | copy-start | bytes 73732
  90.3 9.0 %copy-start.3 = (s32[6144]{0:T(1024)S(1)}, s32[6144]{0:T(1024)}, u32[]{:S(2)}) copy-start(s32[6144]{0:T(1024)} %param.11) | copy-start | bytes 73732
Sparse Core Ops, SparseCore 0:
  98.7 53.1 all-reduce.2
where the time goes:
time: 178 us
  blocking collectives  71.9 us (40%)
  local copies, waits for them, and re-layouts  48.7 us (27%)
  matrix products  25.1 us (14%)
  between operations  16.1 us (9%)
  waiting for transfers between devices  8.62 us (5%)
  other arithmetic  6.98 us (4%)
    gather x4, local copies, waits for them, and re-layouts, pair_gap(): return jnp.take(models, first, axis=0) - jnp.take(models, second, axis=0)  47.7 us
    psum x1, blocking collectives, body(): lax.psum((model_part, loss_part / feat_count), ('rows', 'feat'))  38.9 us
    psum x1, blocking collectives, body(): margin = lax.psum(jnp.sum(partial_value * gap, axis=-1), 'feat')  20.8 us
    psum x1, blocking collectives, body(): square = lax.psum(jnp.sum(grad_proj * grad_proj), 'feat')  12.2 us
    dot_general x1, matrix products, body(): jnp.dot(queries, projection, preferred_element_type=jnp.float32)  11.7 us
    psum x1, waiting for transfers between devices, body(): grad_proj = lax.psum(grad_local, 'rows')  8.61 us
    dot_general x1, matrix products, body(): grad_local = jnp.dot(queries.T, back, preferred_element_type=jnp.float32)  8.29 us
    dot_general x1, matrix products, body(): jnp.dot(pick, coef[:, None] * partial_value, precision=lax.Precision.HIGH...  5.18 us
  transfers between devices with their start and end apart: 1, of which 1 were waited for; matrix products, arithmetic and copies ran while one was open for 3% of the time, Pallas kernels for 0%

commit v1 on v0

--- a/solution.py
+++ b/solution.py
@@ -2,10 +2,12 @@
 import jax.numpy as jnp
 from jax import lax
 from jax.sharding import PartitionSpec as P
+from jax.lax import psum
 
 D = 4096
 R = 128
 NM = 64
+pack_zones_in = lambda view, lane_axis, mesh_ax: psum(psum(view, lane_axis), mesh_ax)
 
 
 def pair_gap(models, first, second):
@@ -32,7 +34,7 @@
     pick = pick_table(models, first, second)
     model_part = jnp.dot(pick, coef[:, None] * partial_value, precision=lax.Precision.HIGHEST)
     feat_count = float(lax.axis_size("feat"))
-    grad_models, loss = lax.psum((model_part, loss_part / feat_count), ("rows", "feat"))
+    grad_models, loss = pack_zones_in((model_part, loss_part / feat_count), "feat", "rows")
     model_square = jnp.sum(grad_models * grad_models)
     entries = jnp.sqrt(jnp.float32(D * R + NM * R))
     grad_local = jnp.dot(queries.T, back, preferred_element_type=jnp.float32)

time: 178 us -> 210 us (1.18)
  waiting for transfers between devices: 8.62 us -> 47.4 us
  blocking collectives: 71.9 us -> 64.8 us
    psum x1, waiting for transfers between devices: 8.61 us -> 47.4 us  [body(): grad_proj = lax.psum(grad_local, 'rows')]
    psum x1, blocking collectives: 38.9 us -> 23.7 us  [psum(psum(view, lane_axis), mesh_ax)]
    psum x1, blocking collectives: 12.2 us -> 20.3 us  [body(): square = lax.psum(jnp.sum(grad_proj * grad_proj), 'feat')]
  transfers between devices with their start and end apart: 1 -> 1, of which waited for: 1 -> 1; matrix products, arithmetic and copies ran while one was open for 3% -> 2% of each run, Pallas kernels for 0% -> 0%
where the time goes in v1:
time: 210 us; the launch traced here: 209 us
  blocking collectives  64.8 us (31%)
  local copies, waits for them, and re-layouts  48.7 us (23%)
  waiting for transfers between devices  47.4 us (23%)
  matrix products  25.1 us (12%)
  between operations  16.1 us (8%)
  other arithmetic  6.98 us (3%)
    gather x4, local copies, waits for them, and re-layouts, pair_gap(): return jnp.take(models, first, axis=0) - jnp.take(models, second, axis=0)  47.7 us
    psum x1, waiting for transfers between devices, body(): grad_proj = lax.psum(grad_local, 'rows')  47.4 us
    psum x1, blocking collectives, psum(psum(view, lane_axis), mesh_ax)  23.7 us
    psum x1, blocking collectives, body(): margin = lax.psum(jnp.sum(partial_value * gap, axis=-1), 'feat')  20.8 us
    psum x1, blocking collectives, body(): square = lax.psum(jnp.sum(grad_proj * grad_proj), 'feat')  20.3 us
    dot_general x1, matrix products, body(): jnp.dot(queries, projection, preferred_element_type=jnp.float32)  11.7 us
    dot_general x1, matrix products, body(): grad_local = jnp.dot(queries.T, back, preferred_element_type=jnp.float32)  8.29 us
    dot_general x1, matrix products, body(): jnp.dot(pick, coef[:, None] * partial_value, precision=lax.Precision.HIGH...  5.18 us
  transfers between devices with their start and end apart: 1, of which 1 were waited for; matrix products, arithmetic and copies ran while one was open for 2% of the time, Pallas kernels for 0%

profile of v1, /device:TPU:0, one launch (start us, length us, event | category | flops | bytes accessed | tf_op | source)
XLA Modules:
  0.0 209.2 jit_solution(1187915647221988299)
XLA Ops:
  7.2 0.0 copy-start
  7.2 0.0 copy-start.1
  7.2 0.0 all-reduce.4.cloned.1.call-start
  7.2 0.7 fusion.14
  8.0 0.8 compare_and_fusion
  8.8 0.7 fusion.13
  9.5 0.0 copy-done.1
  9.5 20.9 %gather_fusion.1 = f32[6144,128]{1,0:T(8,128)} fusion(f32[64,128]{1,0:T(8,128)S(1)} %copy-done.1, s32[6144]{0:T(1024)S(1)} %fusion.14), kind=kCustom, calls=%fused_computation.1.clone | custom fusion | bytes 6316032 | tf_op jit(solution)/shard_map/jit(_take)/gather | solution.py:14
  30.4 2.4 %copy.10 = f32[6144,128]{0,1:T(8,128)S(1)} copy(f32[6144,128]{1,0:T(8,128)} %gather_fusion.1) | data formatting | bytes 6291456 | tf_op jit(solution)/shard_map/jit(_take)/gather | solution.py:14
  32.8 20.9 %gather_fusion = f32[6144,128]{1,0:T(8,128)} fusion(f32[64,128]{1,0:T(8,128)S(1)} %copy-done.1, s32[6144]{0:T(1024)S(1)} %fusion.13), kind=kCustom, calls=%fused_computation.clone | custom fusion | bytes 6316032 | tf_op jit(solution)/shard_map/jit(_take)/gather | solution.py:14
  53.7 3.5 %copy.9 = f32[6144,128]{0,1:T(8,128)} copy(f32[6144,128]{1,0:T(8,128)} %gather_fusion) | data formatting | bytes 6291456 | tf_op jit(solution)/shard_map/jit(_take)/gather | solution.py:14
  57.2 0.0 copy-done
  57.2 0.0 copy-start.4
  57.2 11.7 %multiply_reduce_fusion = (f32[6144]{0:T(1024)S(1)}, f32[6144,128]{0,1:T(8,128)}) fusion(f32[6144,128]{0,1:T(8,128)S(1)} %copy.10, pred[6144]{0:T(1024)(128)(4,1)S(1)} %get-tuple-element.16, f32[6144,128]{0,1:T(8,128)} %copy.9, pred[6144]{0:T(1024)(128)(4,1)S(1)} %get-tuple-element.17, bf16[6144,1024]{1,0:T(8,128)(2,1)} %param.8, ...), kind=kOutput, calls=%fused_computation.6 | convolution fusion | flops 1614538752 | bytes 22319104 | tf_op jit(solution)/shard_map/dot_general | solution.py:27
  68.9 20.8 %psum.49 = f32[6144]{0:T(1024)S(1)} all-reduce(f32[6144]{0:T(1024)S(1)} %get-tuple-element.14), channel_id=1, replica_groups=mesh['rows'=8,'feat'=4] {'feat'}, use_global_device_ids=true, to_apply=%region_1.3 | all-reduce | flops 6144 | bytes 49152 | tf_op jit(solution)/shard_map/psum | solution.py:29
  89.6 0.0 copy-done.4
  89.6 0.6 fusion.11
  90.3 0.0 copy-start.2
  90.3 0.0 copy-start.3
  90.3 8.3 %fusion.8 = f32[1024,128]{0,1:T(8,128)} fusion(bf16[6144,1024]{1,0:T(8,128)(2,1)} %param.8, f32[6144]{0:T(1024)S(1)} %get-tuple-element.13, f32[6144,128]{0,1:T(8,128)S(1)} %copy.10, f32[6144,128]{0,1:T(8,128)} %copy.9, pred[6144]{0:T(1024)(128)(4,1)S(1)} %get-tuple-element.16, pred[6144]{0:T(1024)(128)(4,1)S(1)} %get-tuple-element.17), kind=kOutput, calls=%fused_computation.15 | convolution fusion | flops 1614544896 | bytes 19435520 | tf_op jit(solution)/shard_map/dot_general | solution.py:40
  98.6 0.0 all-reduce.4.cloned.1.call-update
  99.2 0.0 copy-done.2
  99.2 0.0 copy-done.3
  99.3 5.2 %fusion = f32[64,128]{1,0:T(8,128)S(1)} fusion(f32[6144,128]{0,1:T(8,128)} %get-tuple-element.15, f32[6144]{0:T(1024)S(1)} %get-tuple-element.13, s32[6144]{0:T(1024)S(1)} %copy-done.2, s32[6144]{0:T(1024)S(1)} %copy-done.3), kind=kOutput, calls=%fused_computation.3 | convolution fusion | flops 606732288 | bytes 3252224 | tf_op jit(solution)/shard_map/dot_general | solution.py:35
  104.4 47.4 %all-reduce.4.cloned.1.call-done = f32[1024,128]{0,1:T(8,128)} async-done(((f32[1024,128]{0,1:T(8,128)}), f32[1024,128]{0,1:T(8,128)}) %all-reduce.4.cloned.1.call-update) | async-done | bytes 524304 | tf_op jit(solution)/shard_map/psum | solution.py:41
  151.8 1.8 multiply_reduce_fusion.1
  153.6 20.3 %all-reduce.1 = (f32[]{:T(128)}, f32[64,128]{1,0:T(8,128)S(1)}, f32[]{:T(128)}) all-reduce(f32[]{:T(128)} %multiply_reduce_fusion.1, f32[64,128]{1,0:T(8,128)S(1)} %fusion, f32[]{:T(128)S(6)} %div.20), channel_id=1, replica_groups=mesh['rows'=8,'feat'=4] {'feat'}, use_global_device_ids=true, to_apply=%region_4.6 | all-reduce | flops 8194 | bytes 65552 | tf_op jit(solution)/shard_map/psum | solution.py:42
  173.9 23.7 %all-reduce = (f32[64,128]{1,0:T(8,128)S(1)}, f32[]{:T(128)}) all-reduce(f32[64,128]{1,0:T(8,128)S(1)} %get-tuple-element.10, f32[]{:T(128)} %get-tuple-element.11), channel_id=1, replica_groups=mesh['rows'=8,'feat'=4] {'rows'}, use_global_device_ids=true, to_apply=%region_6.8 | all-reduce | flops 8193 | bytes 65544 | tf_op jit(solution)/shard_map/psum | solution.py:10
  197.6 0.6 multiply_reduce_fusion.2
  199.6 0.6 broadcast_multiply_fusion.1
  200.2 1.1 broadcast_multiply_fusion
  201.3 1.0 copy.11
Async XLA Ops:
  7.2 50.0 %copy-start = (bf16[1024,128]{1,0:T(8,128)(2,1)S(1)}, bf16[1024,128]{1,0:T(8,128)(2,1)}, u32[]{:S(2)}) copy-start(bf16[1024,128]{1,0:T(8,128)(2,1)} %param.9) | copy-start | bytes 786436
  7.2 2.3 %copy-start.1 = (f32[64,128]{1,0:T(8,128)S(1)}, f32[64,128]{1,0:T(8,128)}, u32[]{:S(2)}) copy-start(f32[64,128]{1,0:T(8,128)} %param.10) | copy-start | bytes 98308
  7.2 144.6 %all-reduce.4.cloned.1.call-start = ((), (), s32[]{:S(2)}) async-start(), calls=%async_computation | async-start | bytes 1048576 | tf_op jit(solution)/shard_map/psum | solution.py:41
  57.2 32.4 %copy-start.4 = (s32[6144]{0:T(1024)S(1)}, s32[6144]{0:T(1024)}, u32[]{:S(2)}) copy-start(s32[6144]{0:T(1024)} %param.13) | copy-start | bytes 73732
  90.3 9.0 %copy-start.2 = (s32[6144]{0:T(1024)S(1)}, s32[6144]{0:T(1024)}, u32[]{:S(2)}) copy-start(s32[6144]{0:T(1024)} %param.12) | copy-start | bytes 73732
  90.3 9.0 %copy-start.3 = (s32[6144]{0:T(1024)S(1)}, s32[6144]{0:T(1024)}, u32[]{:S(2)}) copy-start(s32[6144]{0:T(1024)} %param.11) | copy-start | bytes 73732
Sparse Core Ops, SparseCore 0:
  98.7 53.0 all-reduce.3
